TPU v7x, 128 devices: a whole 4x4x4 slice. The times are simulated.
128 devices in a mesh: quad: 8 (over z, x_lo), row: 16 (over x_hi, y, core).
Axes of the slice: x: 4 (x_hi: 2, x_lo: 2; x = x_hi * 2 + x_lo), y: 4, z: 4, core: 2. Of those that a mesh axis runs over, the one named last changes fastest.
Arguments:
- hamiltonian: bfloat16 [1024, 64, 1536], P('row'), may hold values from -0.15625 to 0.15625
- columns: int32 [1024, 24], P('row'), may hold values from 0 to 1023, as said below
- counts: int32 [1024], P('row'), may hold values from 2 to 24, as said below
- precond: bfloat16 [16, 1024, 64, 128], P('quad', 'row'), may hold values from -0.5 to 0.5
- rhs: bfloat16 [65536, 128], P('row'), may hold values from -6 to 6
Outputs:
- moments_out: float32 [8, 65536, 128], P('quad', 'row')
- blocks_out: float32 [8, 128, 128], P('quad')
Inputs may be any that keep to these rules, and one draw needn't show every extreme that they name: `columns`: slot 0 of row block b holds b itself; slot 1 holds b - 64 for even b and b + 64 for odd b, reflected at the ends (an index -m becomes m, an index 1023 + m becomes 1024 - 1 - m); every column block lies within 64 blocks of its row block. `counts`: every run of 64 row blocks starting at a multiple of 64 holds a row block with all 24 slots live.
All inputs are finite; a program needn't handle non-finite values.
Results may differ from a plain program's by a relative error of at most 0.02.
Values may be sent and summed in bfloat16 or wider, within the bound.
No kernel may reach another device: no remote copies, remote signals or barrier semaphores. Data moves between devices by JAX's collectives and lax.ppermute only.
A program may use at most 128 MiB of HBM per device.

v0:
```python
import math
import jax
import jax.numpy as jnp
from jax import lax
from jax.sharding import PartitionSpec as P

ITERS = 2
MOMENTS = 8


def extended_2(x, sides, width):
    for axis, dim in sides:
        peers, length = (lax.axis_size(axis), x.shape[dim])
        up = [(i, (i + 1) % peers) for i in range(peers - 1)]
        down = [(j, i) for i, j in up]
        last = lax.slice_in_dim(x, length - width, length, axis=dim)
        first = lax.slice_in_dim(x, 0, width, axis=dim)
        before = lax.ppermute(last, axis, up)
        after = lax.ppermute(first, axis, down)
        x = jnp.concatenate([before, x, after], axis=dim)
    return x


def rotate(values):
    half_cols = values.shape[-1] // 2
    return jnp.concatenate([-values[..., half_cols:], values[..., :half_cols]], axis=-1)


def precondition(blocks_pre, resid):
    stacked = jnp.concatenate([resid, rotate(resid)], axis=1)
    return jnp.einsum("bij,bjc->bic", blocks_pre, stacked, preferred_element_type=jnp.float32)


def shards(hamiltonian, columns, counts, precond, rhs):
    row_blocks = hamiltonian.shape[0]
    block_size = hamiltonian.shape[1]
    slots = columns.shape[1]
    width = rhs.shape[1]
    per_quad = precond.shape[0]
    quad_count = lax.axis_size("quad")
    row_count = lax.axis_size("row")
    quads_total = per_quad * quad_count
    per_device = MOMENTS // quad_count
    local_rows = row_blocks * block_size
    row_index = lax.axis_index("row")
    quad_index = lax.axis_index("quad")
    first_block = (row_index - 1) * row_blocks
    live = jnp.arange(slots)[None, :] < counts[:, None]
    local_index = jnp.where(live, columns - first_block, 3 * row_blocks)
    rhs_blocks = rhs.reshape(row_blocks, block_size, width)
    rhs_float = rhs_blocks.astype(jnp.float32)
    thetas = []
    solutions = []
    for which in range(per_quad):
        theta = (
            2.0 * jnp.pi * ((quad_index * per_quad + which).astype(jnp.float32) + 0.5) / quads_total
        )
        thetas.append(theta)
        zreal = jnp.cos(theta)
        zimag = jnp.sin(theta)
        iterate = precondition(precond[which], rhs_blocks).astype(jnp.bfloat16)
        for sweep in range(ITERS):
            flat = iterate.reshape(local_rows, width)
            extended = extended_2(flat, (("row", 0),), local_rows)
            stacked = jnp.concatenate(
                [
                    extended.reshape(3 * row_blocks, block_size, width),
                    jnp.zeros((1, block_size, width), jnp.bfloat16),
                ],
                axis=0,
            )
            gathered = stacked[local_index].reshape(row_blocks, slots * block_size, width)
            product = jnp.einsum(
                "bij,bjc->bic", hamiltonian, gathered, preferred_element_type=jnp.float32
            )
            current = iterate.astype(jnp.float32)
            shifted = zreal * current + zimag * rotate(current)
            resid = (rhs_float - (shifted - product)).astype(jnp.bfloat16)
            iterate = (current + precondition(precond[which], resid)).astype(jnp.bfloat16)
        solutions.append(iterate.reshape(local_rows, width))
    orders = jnp.arange(lax.axis_size("quad") * per_device).astype(jnp.float32) + 1.0
    total = jnp.zeros((lax.axis_size("quad") * per_device, local_rows, width), jnp.float32)
    for which in range(per_quad):
        phase = orders * thetas[which]
        coef_a = jnp.cos(phase) / quads_total
        coef_b = jnp.sin(phase) / quads_total
        current = solutions[which].astype(jnp.float32)
        total = (
            total
            + coef_a[:, None, None] * current[None]
            + coef_b[:, None, None] * rotate(current)[None]
        )
    held = lax.optimization_barrier(total.astype(jnp.bfloat16))
    moments_out = lax.psum_scatter(
        held.astype(jnp.float32).astype(jnp.bfloat16), "quad", scatter_dimension=0, tiled=True
    ).astype(jnp.float32)
    scale = 1.0 / math.sqrt(local_rows * row_count)
    flat_rhs = rhs.astype(jnp.float32)
    local_blocks = (
        jnp.einsum("rc,krd->kcd", flat_rhs, moments_out, precision=lax.Precision.HIGHEST) * scale
    )
    blocks_out = lax.psum(local_blocks.astype(jnp.bfloat16), "row").astype(jnp.float32)
    return (moments_out, blocks_out)


def solution(mesh):
    return jax.shard_map(
        shards,
        mesh=mesh,
        in_specs=(
            P("row", None, None),
            P("row", None),
            P("row"),
            P("quad", "row", None, None),
            P("row", None),
        ),
        out_specs=(P("quad", "row", None), P("quad", None, None)),
        check_vma=False,
    )
```

profile of v0, /device:TPU:0, one launch (start us, length us, event | category | flops | bytes accessed | tf_op | source)
XLA Modules:
  0.0 562.5 jit_solution(10902191708547151597)
XLA Ops:
  7.2 2.1 slice_negate_fusion.10
  10.5 2.5 collective-permute-start.4
  14.3 2.5 bitcast_convert_fusion.3
  16.8 4.9 collective-permute-start
  24.7 2.8 slice_negate_fusion.2
  27.6 2.8 slice_negate_fusion.5
  30.4 8.6 %pad_maximum_fusion.2 = bf16[12288,128]{1,0:T(8,128)(2,1)S(1)} fusion(bf16[4096,128]{1,0:T(8,128)(2,1)} %collective-permute-done.5, bf16[4096,128]{1,0:T(8,128)(2,1)S(1)} %bitcast.108, bf16[4096,128]{1,0:T(8,128)(2,1)} %collective-permute-done.4), kind=kLoop, calls=%fused_computation.11 | loop fusion | flops 9437184 | bytes 6291456 | tf_op jit(solution)/shard_map/concatenate | solution.py:20
  39.7 32.0 %gather_fusion.2 = bf16[1536,64,128]{2,1,0:T(8,128)(2,1)} fusion(bf16[193,64,128]{2,1,0:T(8,128)(2,1)S(1)} %concatenate.89, s32[2048]{0:T(1024)S(1)} %pad_clamp_fusion), kind=kCustom, calls=%fused_computation.2 | custom fusion | bytes 50337792 | tf_op jit(solution)/shard_map/gather | solution.py:72
  71.8 16.3 %fusion.2 = bf16[64,64,128]{2,1,0:T(8,128)(2,1)S(1)} fusion(bf16[64,64,128]{2,1,0:T(8,128)(2,1)} %bitcast.100, f32[64,64,64]{2,1,0:T(8,128)} %get-tuple-element.13, f32[64,64,64]{2,1,0:T(8,128)} %get-tuple-element.12, bf16[64,64,1536]{2,1,0:T(8,128)(2,1)} %param.5, bf16[64,1536,128]{2,1,0:T(8,128)(2,1)} %bitcast.97, bf16[64,128,64]{1,2,0:T(8,128)(2,1)} %copy-done.5, ...), kind=kOutput, calls=%fused_computation.15 | convolution fusion | flops 1615331328 | bytes 42991624 | tf_op jit(solution)/shard_map/bij,bjc->bic/dot_general | solution.py:73
  90.0 2.6 fusion.71
  92.6 4.3 collective-permute-start.6
  98.2 4.1 pad_maximum_fusion
  103.1 32.0 %gather_fusion = bf16[1536,64,128]{2,1,0:T(8,128)(2,1)} fusion(bf16[193,64,128]{2,1,0:T(8,128)(2,1)S(1)} %concatenate.78, s32[2048]{0:T(1024)S(1)} %pad_clamp_fusion), kind=kCustom, calls=%fused_computation | custom fusion | bytes 50337792 | tf_op jit(solution)/shard_map/gather | solution.py:72
  135.1 16.1 %fusion = bf16[64,64,128]{2,1,0:T(8,128)(2,1)S(1)} fusion(bf16[64,64,128]{2,1,0:T(8,128)(2,1)} %bitcast.101, f32[64,64,64]{2,1,0:T(8,128)} %get-tuple-element.9, f32[64,64,64]{2,1,0:T(8,128)} %get-tuple-element.8, bf16[64,64,1536]{2,1,0:T(8,128)(2,1)} %param.5, bf16[64,1536,128]{2,1,0:T(8,128)(2,1)} %bitcast.98, ...), kind=kOutput, calls=%fused_computation.13 | convolution fusion | flops 1615331328 | bytes 42991624 | tf_op jit(solution)/shard_map/bij,bjc->bic/dot_general | solution.py:73
  151.6 3.0 slice.127
  154.6 3.1 fusion.72
  157.7 4.2 collective-permute-start.2
  163.7 2.8 slice.117
  166.4 1.9 slice_negate_fusion.1
  168.4 2.0 slice_negate_fusion.4
  170.4 4.1 pad_maximum_fusion.3
  175.2 32.0 %gather_fusion.3 = bf16[1536,64,128]{2,1,0:T(8,128)(2,1)} fusion(bf16[193,64,128]{2,1,0:T(8,128)(2,1)S(1)} %concatenate.94, s32[2048]{0:T(1024)S(1)} %pad_clamp_fusion), kind=kCustom, calls=%fused_computation.3 | custom fusion | bytes 50337792 | tf_op jit(solution)/shard_map/gather | solution.py:72
  207.3 16.1 %fusion.3 = bf16[64,64,128]{2,1,0:T(8,128)(2,1)S(1)} fusion(bf16[64,64,128]{2,1,0:T(8,128)(2,1)} %bitcast.102, f32[64,64,64]{2,1,0:T(8,128)} %slice.127, f32[64,64,64]{2,1,0:T(8,128)} %slice_negate_fusion.1, bf16[64,64,1536]{2,1,0:T(8,128)(2,1)} %param.5, bf16[64,1536,128]{2,1,0:T(8,128)(2,1)} %bitcast.96, bf16[64,64,128]{2,1,0:T(8,128)(2,1)} %get-tuple-element.27, ...), kind=kOutput, calls=%fused_computation.16 | convolution fusion | flops 1615331328 | bytes 42991624 | tf_op jit(solution)/shard_map/bij,bjc->bic/dot_general | solution.py:73
  225.0 2.1 fusion.36
  227.3 2.7 slice_negate_fusion
  230.0 4.3 pad_maximum_fusion.1
  235.0 32.0 %gather_fusion.1 = bf16[1536,64,128]{2,1,0:T(8,128)(2,1)} fusion(bf16[193,64,128]{2,1,0:T(8,128)(2,1)S(1)} %concatenate.83, s32[2048]{0:T(1024)S(1)} %pad_clamp_fusion), kind=kCustom, calls=%fused_computation.1 | custom fusion | bytes 50337792 | tf_op jit(solution)/shard_map/gather | solution.py:72
  267.1 16.4 %fusion.1 = bf16[64,64,128]{2,1,0:T(8,128)(2,1)S(1)} fusion(bf16[64,64,128]{2,1,0:T(8,128)(2,1)} %bitcast.103, f32[64,64,64]{2,1,0:T(8,128)} %slice.117, f32[64,64,64]{2,1,0:T(8,128)} %slice_negate_fusion.4, bf16[64,64,1536]{2,1,0:T(8,128)(2,1)} %param.5, bf16[64,1536,128]{2,1,0:T(8,128)(2,1)} %bitcast.95, bf16[64,64,128]{2,1,0:T(8,128)(2,1)} %get-tuple-element.31, ...), kind=kOutput, calls=%fused_computation.14 | convolution fusion | flops 1615331328 | bytes 42991624 | tf_op jit(solution)/shard_map/bij,bjc->bic/dot_general | solution.py:73
  285.1 2.1 fusion.38
  291.2 6.1 %add_convert_fusion = bf16[8,4096,128]{2,1,0:T(8,128)(2,1)} fusion(f32[4096,128]{1,0:T(8,128)S(1)} %get-tuple-element.37, f32[8]{0:T(128)S(1)} %copy-done.17, f32[4096,128]{1,0:T(8,128)S(1)} %copy-done.3, f32[8]{0:T(128)S(1)} %copy-done.18, f32[4096,128]{1,0:T(8,128)S(1)} %get-tuple-element.36, f32[8]{0:T(128)S(1)} %copy-done.19, ...), kind=kLoop, calls=%fused_computation.4 | loop fusion | flops 33554432 | bytes 16777344 | tf_op jit(solution)/shard_map/convert_element_type | solution.py:93
  297.4 185.1 %reduce-scatter.2.cloned.1.call-done = bf16[1,4096,128]{2,1,0:T(8,128)(2,1)} async-done(((bf16[8,4096,128]{2,1,0:T(8,128)(2,1)}), bf16[1,4096,128]{2,1,0:T(8,128)(2,1)}) %reduce-scatter.2.cloned.1.call-update) | async-done | bytes 1048592 | tf_op jit(solution)/shard_map/reduce_scatter | solution.py:94
  484.2 69.1 %psum.7 = bf16[1,128,128]{1,2,0:T(8,128)(2,1)S(1)} all-reduce(bf16[1,128,128]{1,2,0:T(8,128)(2,1)S(1)} %fusion.49), channel_id=1, replica_groups=mesh['quad'=8,'row'=16] {'row'}, use_global_device_ids=true, to_apply=%region_1.2 | all-reduce | flops 16384 | bytes 65536 | tf_op jit(solution)/shard_map/psum | solution.py:102
  (80 shorter events, 24.6 us)
Async XLA Ops:
  7.2 475.2 %reduce-scatter.2.cloned.1.call-start = ((), (), s32[]{:S(2)}) async-start(), calls=%async_computation.1 | async-start | bytes 9437184 | tf_op jit(solution)/shard_map/reduce_scatter | solution.py:94
  7.2 2.2 copy-start
  7.2 2.5 copy-start.8
  10.5 19.9 %copy-start.5 = (bf16[64,128,64]{1,2,0:T(8,128)(2,1)}, bf16[64,128,64]{1,2,0:T(8,128)(2,1)S(1)}, u32[]{:S(2)}) copy-start(bf16[64,128,64]{1,2,0:T(8,128)(2,1)S(1)} %get-tuple-element.25) | copy-start | bytes 3145732
  10.5 12.8 %copy-start.16 = (s32[64,24]{0,1:T(8,128)S(1)}, s32[64,24]{0,1:T(8,128)}, u32[]{:S(2)}) copy-start(s32[64,24]{0,1:T(8,128)} %param.6) | copy-start | bytes 18436
  10.5 12.8 %copy-start.21 = (s32[64]{0:T(128)S(1)}, s32[64]{0:T(128)}, u32[]{:S(2)}) copy-start(s32[64]{0:T(128)} %param.7) | copy-start | bytes 772
  10.5 19.8 %collective-permute-start.4 = (bf16[4096,128]{1,0:T(8,128)(2,1)S(1)}, bf16[4096,128]{1,0:T(8,128)(2,1)}, u32[]{:S(2)}, u32[]{:S(2)}) collective-permute-start(bf16[4096,128]{1,0:T(8,128)(2,1)S(1)} %bitcast.106), channel_id=1, source_target_pairs={{0,1},{1,2},{2,3},{3,4},{4,5},{5,6},{6,7},{7,8},{8,9},{9,10},{10,1... | collective-permute-start | bytes 3145736 | tf_op jit(solution)/shard_map/ppermute | solution.py:18
  13.0 17.4 %collective-permute-start.5 = (bf16[4096,128]{1,0:T(8,128)(2,1)S(1)}, bf16[4096,128]{1,0:T(8,128)(2,1)}, u32[]{:S(2)}, u32[]{:S(2)}) collective-permute-start(bf16[4096,128]{1,0:T(8,128)(2,1)S(1)} %bitcast.107), channel_id=1, source_target_pairs={{1,0},{2,1},{3,2},{4,3},{5,4},{6,5},{7,6},{8,7},{9,8},{10,9},{11,1... | collective-permute-start | bytes 3145736 | tf_op jit(solution)/shard_map/ppermute | solution.py:19
  16.8 81.4 %collective-permute-start = (bf16[4096,128]{1,0:T(8,128)(2,1)}, bf16[4096,128]{1,0:T(8,128)(2,1)}, u32[]{:S(2)}, u32[]{:S(2)}) collective-permute-start(bf16[4096,128]{1,0:T(8,128)(2,1)} %bitcast.3), channel_id=1, source_target_pairs={{0,1},{1,2},{2,3},{3,4},{4,5},{5,6},{6,7},{7,8},{8,9},{9,10},{10,1... | collective-permute-start | bytes 3145736 | tf_op jit(solution)/shard_map/ppermute | solution.py:18
  21.7 76.5 %collective-permute-start.1 = (bf16[4096,128]{1,0:T(8,128)(2,1)}, bf16[4096,128]{1,0:T(8,128)(2,1)}, u32[]{:S(2)}, u32[]{:S(2)}) collective-permute-start(bf16[4096,128]{1,0:T(8,128)(2,1)} %bitcast.3), channel_id=1, source_target_pairs={{1,0},{2,1},{3,2},{4,3},{5,4},{6,5},{7,6},{8,7},{9,8},{10,9},{11,1... | collective-permute-start | bytes 3145736 | tf_op jit(solution)/shard_map/ppermute | solution.py:19
  24.7 2.8 copy-start.4
  88.1 1.2 copy-start.6
  88.1 1.9 copy-start.9
  92.6 77.8 %collective-permute-start.6 = (bf16[4096,128]{1,0:T(8,128)(2,1)}, bf16[4096,128]{1,0:T(8,128)(2,1)}, u32[]{:S(2)}, u32[]{:S(2)}) collective-permute-start(bf16[4096,128]{1,0:T(8,128)(2,1)} %bitcast.24), channel_id=1, source_target_pairs={{0,1},{1,2},{2,3},{3,4},{4,5},{5,6},{6,7},{7,8},{8,9},{9,10},{10,1... | collective-permute-start | bytes 3145736 | tf_op jit(solution)/shard_map/ppermute | solution.py:18
  96.9 73.5 %collective-permute-start.7 = (bf16[4096,128]{1,0:T(8,128)(2,1)}, bf16[4096,128]{1,0:T(8,128)(2,1)}, u32[]{:S(2)}, u32[]{:S(2)}) collective-permute-start(bf16[4096,128]{1,0:T(8,128)(2,1)} %bitcast.24), channel_id=1, source_target_pairs={{1,0},{2,1},{3,2},{4,3},{5,4},{6,5},{7,6},{8,7},{9,8},{10,9},{11,1... | collective-permute-start | bytes 3145736 | tf_op jit(solution)/shard_map/ppermute | solution.py:19
  151.6 3.0 copy-start.10
  157.7 8.7 %copy-start.7 = (f32[64,64,128]{2,1,0:T(8,128)S(1)}, f32[64,64,128]{2,1,0:T(8,128)}, u32[]{:S(2)}) copy-start(f32[64,64,128]{2,1,0:T(8,128)} %get-tuple-element.26) | copy-start | bytes 6291460
  157.7 72.3 %collective-permute-start.2 = (bf16[4096,128]{1,0:T(8,128)(2,1)}, bf16[4096,128]{1,0:T(8,128)(2,1)}, u32[]{:S(2)}, u32[]{:S(2)}) collective-permute-start(bf16[4096,128]{1,0:T(8,128)(2,1)} %bitcast.9), channel_id=1, source_target_pairs={{0,1},{1,2},{2,3},{3,4},{4,5},{5,6},{6,7},{7,8},{8,9},{9,10},{10,1... | collective-permute-start | bytes 3145736 | tf_op jit(solution)/shard_map/ppermute | solution.py:18
  162.0 68.0 %collective-permute-start.3 = (bf16[4096,128]{1,0:T(8,128)(2,1)}, bf16[4096,128]{1,0:T(8,128)(2,1)}, u32[]{:S(2)}, u32[]{:S(2)}) collective-permute-start(bf16[4096,128]{1,0:T(8,128)(2,1)} %bitcast.9), channel_id=1, source_target_pairs={{1,0},{2,1},{3,2},{4,3},{5,4},{6,5},{7,6},{8,7},{9,8},{10,9},{11,1... | collective-permute-start | bytes 3145736 | tf_op jit(solution)/shard_map/ppermute | solution.py:19
  223.4 1.6 copy-start.11
  227.3 2.7 copy-start.2
  283.5 1.6 copy-start.12
  287.4 1.6 copy-start.13
  287.4 2.2 copy-start.14
  289.6 1.6 copy-start.3
  289.6 1.6 copy-start.17
  289.6 1.6 copy-start.18
  289.6 1.6 copy-start.19
  289.6 1.6 copy-start.20
  297.3 185.1 %copy-start.1 = (bf16[4096,128]{1,0:T(8,128)(2,1)S(1)}, bf16[4096,128]{1,0:T(8,128)(2,1)}, u32[]{:S(2)}) copy-start(bf16[4096,128]{1,0:T(8,128)(2,1)} %param.9) | copy-start | bytes 3145732
  482.4 71.6 %copy-start.15 = (bf16[1,4096,128]{2,1,0:T(8,128)(2,1)S(1)}, bf16[1,4096,128]{2,1,0:T(8,128)(2,1)}, u32[]{:S(2)}) copy-start(bf16[1,4096,128]{2,1,0:T(8,128)(2,1)} %reduce-scatter.2.cloned.1.call-done) | copy-start | bytes 3145732
Sparse Core Ops, SparseCore 0:
  297.5 184.8 reduce-scatter.1
where the time goes:
time: 567 us; the launch traced here: 563 us
  waiting for transfers between devices  185 us (33%)
  local copies, waits for them, and re-layouts  144 us (25%)
  matrix products  79.8 us (14%)
  blocking collectives  69.1 us (12%)
  other arithmetic  48.4 us (9%)
  starting transfers between devices  21.5 us (4%)
  between operations  15 us (3%)
    reduce_scatter x1, waiting for transfers between devices, shards(): lax.psum_scatter(held.astype(jnp.float32).astype(jnp.bfloat16), 'quad', s...  185 us
    gather x4, local copies, waits for them, and re-layouts, shards(): stacked[local_index].reshape(row_blocks, slots * block_size, width)  128 us
    psum x1, blocking collectives, shards(): lax.psum(local_blocks.astype(jnp.bfloat16), 'row').astype(jnp.float32)  69.1 us
    dot_general x4, matrix products, shards(): jnp.einsum('bij,bjc->bic', hamiltonian, gathered, preferred_element_type=...  64.9 us
    concatenate x4, other arithmetic, extended_2(): x = jnp.concatenate([before, x, after], axis=dim)  21.2 us
    neg x11, other arithmetic, rotate(): -values[..., half_cols:]  16.8 us
    ppermute x4, starting transfers between devices, extended_2(): before = lax.ppermute(last, axis, up)  15.9 us
    dot_general x6, matrix products, precondition(): jnp.einsum('bij,bjc->bic', blocks_pre, stacked, preferred_element_type=jn...  13.1 us
  transfers between devices with their start and end apart: 9, of which 1 were waited for; matrix products, arithmetic and copies ran while one was open for 35% of the time, Pallas kernels for 0%

commit v1 on v0

--- a/solution.py
+++ b/solution.py
@@ -1,3 +1,4 @@
+import functools
 import math
 import jax
 import jax.numpy as jnp
@@ -6,6 +7,13 @@
 
 ITERS = 2
 MOMENTS = 8
+
+
+def divide_points(w_in, mesh_name):
+    return jnp.sum(jax.lax.all_gather(w_in, mesh_name), axis=0)
+
+
+scan_the_tiles = functools.partial(divide_points, mesh_name="row")
 
 
 def extended_2(x, sides, width):
@@ -99,7 +107,7 @@
     local_blocks = (
         jnp.einsum("rc,krd->kcd", flat_rhs, moments_out, precision=lax.Precision.HIGHEST) * scale
     )
-    blocks_out = lax.psum(local_blocks.astype(jnp.bfloat16), "row").astype(jnp.float32)
+    blocks_out = scan_the_tiles(local_blocks.astype(jnp.bfloat16)).astype(jnp.float32)
     return (moments_out, blocks_out)
 
 

time: 567 us -> 524 us (0.924)
  blocking collectives: 69.1 us -> 25.2 us
    psum x1 -> x0, blocking collectives: 69.1 us -> none  [shards(): lax.psum(local_blocks.astype(jnp.bfloat16), 'row').astype(jnp.float32)]
    all_gather x0 -> x1, blocking collectives: none -> 25.2 us  [divide_points(): return jnp.sum(jax.lax.all_gather(w_in, mesh_name), axis=0)]
  transfers between devices with their start and end apart: 9 -> 9, of which waited for: 1 -> 1; matrix products, arithmetic and copies ran while one was open for 35% -> 38% of each run, Pallas kernels for 0% -> 0%
where the time goes in v1:
time: 524 us; the launch traced here: 519 us
  waiting for transfers between devices  185 us (35%)
  local copies, waits for them, and re-layouts  144 us (27%)
  matrix products  79.8 us (15%)
  other arithmetic  48.5 us (9%)
  blocking collectives  25.2 us (5%)
  starting transfers between devices  21.5 us (4%)
  between operations  15 us (3%)
    reduce_scatter x1, waiting for transfers between devices, shards(): lax.psum_scatter(held.astype(jnp.float32).astype(jnp.bfloat16), 'quad', s...  185 us
    gather x4, local copies, waits for them, and re-layouts, shards(): stacked[local_index].reshape(row_blocks, slots * block_size, width)  128 us
    dot_general x4, matrix products, shards(): jnp.einsum('bij,bjc->bic', hamiltonian, gathered, preferred_element_type=...  64.9 us
    all_gather x1, blocking collectives, divide_points(): return jnp.sum(jax.lax.all_gather(w_in, mesh_name), axis=0)  25.2 us
    concatenate x4, other arithmetic, extended_2(): x = jnp.concatenate([before, x, after], axis=dim)  21.2 us
    neg x11, other arithmetic, rotate(): -values[..., half_cols:]  16.8 us
    ppermute x4, starting transfers between devices, extended_2(): before = lax.ppermute(last, axis, up)  15.9 us
    dot_general x6, matrix products, precondition(): jnp.einsum('bij,bjc->bic', blocks_pre, stacked, preferred_element_type=jn...  13.1 us
  transfers between devices with their start and end apart: 9, of which 1 were waited for; matrix products, arithmetic and copies ran while one was open for 38% of the time, Pallas kernels for 0%

profile of v1, /device:TPU:0, one launch (start us, length us, event | category | flops | bytes accessed | tf_op | source)
XLA Modules:
  0.0 519.0 jit_solution(16007697086097431848)
XLA Ops:
  7.2 2.1 slice_negate_fusion.10
  10.5 2.5 collective-permute-start.4
  14.3 2.5 bitcast_convert_fusion.3
  16.8 4.9 collective-permute-start
  24.7 2.8 slice_negate_fusion.2
  27.6 2.8 slice_negate_fusion.5
  30.4 8.6 %pad_maximum_fusion.2 = bf16[12288,128]{1,0:T(8,128)(2,1)S(1)} fusion(bf16[4096,128]{1,0:T(8,128)(2,1)} %collective-permute-done.5, bf16[4096,128]{1,0:T(8,128)(2,1)S(1)} %bitcast.111, bf16[4096,128]{1,0:T(8,128)(2,1)} %collective-permute-done.4), kind=kLoop, calls=%fused_computation.11 | loop fusion | flops 9437184 | bytes 6291456 | tf_op jit(solution)/shard_map/concatenate | solution.py:28
  39.7 32.0 %gather_fusion.2 = bf16[1536,64,128]{2,1,0:T(8,128)(2,1)} fusion(bf16[193,64,128]{2,1,0:T(8,128)(2,1)S(1)} %concatenate.89, s32[2048]{0:T(1024)S(1)} %pad_clamp_fusion), kind=kCustom, calls=%fused_computation.2 | custom fusion | bytes 50337792 | tf_op jit(solution)/shard_map/gather | solution.py:80
  71.8 16.3 %fusion.2 = bf16[64,64,128]{2,1,0:T(8,128)(2,1)S(1)} fusion(bf16[64,64,128]{2,1,0:T(8,128)(2,1)} %bitcast.103, f32[64,64,64]{2,1,0:T(8,128)} %get-tuple-element.11, f32[64,64,64]{2,1,0:T(8,128)} %get-tuple-element.10, bf16[64,64,1536]{2,1,0:T(8,128)(2,1)} %param.5, bf16[64,1536,128]{2,1,0:T(8,128)(2,1)} %bitcast.100, bf16[64,128,64]{1,2,0:T(8,128)(2,1)} %copy-done.5, ...), kind=kOutput, calls=%fused_computation.15 | convolution fusion | flops 1615331328 | bytes 42991624 | tf_op jit(solution)/shard_map/bij,bjc->bic/dot_general | solution.py:81
  90.0 2.6 fusion.71
  92.6 4.3 collective-permute-start.6
  98.2 4.1 pad_maximum_fusion
  103.1 32.0 %gather_fusion = bf16[1536,64,128]{2,1,0:T(8,128)(2,1)} fusion(bf16[193,64,128]{2,1,0:T(8,128)(2,1)S(1)} %concatenate.78, s32[2048]{0:T(1024)S(1)} %pad_clamp_fusion), kind=kCustom, calls=%fused_computation | custom fusion | bytes 50337792 | tf_op jit(solution)/shard_map/gather | solution.py:80
  135.1 16.1 %fusion = bf16[64,64,128]{2,1,0:T(8,128)(2,1)S(1)} fusion(bf16[64,64,128]{2,1,0:T(8,128)(2,1)} %bitcast.104, f32[64,64,64]{2,1,0:T(8,128)} %get-tuple-element.7, f32[64,64,64]{2,1,0:T(8,128)} %get-tuple-element.6, bf16[64,64,1536]{2,1,0:T(8,128)(2,1)} %param.5, bf16[64,1536,128]{2,1,0:T(8,128)(2,1)} %bitcast.101, ...), kind=kOutput, calls=%fused_computation.13 | convolution fusion | flops 1615331328 | bytes 42991624 | tf_op jit(solution)/shard_map/bij,bjc->bic/dot_general | solution.py:81
  151.6 3.0 slice.127
  154.6 3.1 fusion.72
  157.7 4.2 collective-permute-start.2
  163.7 2.8 slice.117
  166.4 1.9 slice_negate_fusion.1
  168.4 2.0 slice_negate_fusion.4
  170.4 4.1 pad_maximum_fusion.3
  175.2 32.0 %gather_fusion.3 = bf16[1536,64,128]{2,1,0:T(8,128)(2,1)} fusion(bf16[193,64,128]{2,1,0:T(8,128)(2,1)S(1)} %concatenate.94, s32[2048]{0:T(1024)S(1)} %pad_clamp_fusion), kind=kCustom, calls=%fused_computation.3 | custom fusion | bytes 50337792 | tf_op jit(solution)/shard_map/gather | solution.py:80
  207.3 16.1 %fusion.3 = bf16[64,64,128]{2,1,0:T(8,128)(2,1)S(1)} fusion(bf16[64,64,128]{2,1,0:T(8,128)(2,1)} %bitcast.105, f32[64,64,64]{2,1,0:T(8,128)} %slice.127, f32[64,64,64]{2,1,0:T(8,128)} %slice_negate_fusion.1, bf16[64,64,1536]{2,1,0:T(8,128)(2,1)} %param.5, bf16[64,1536,128]{2,1,0:T(8,128)(2,1)} %bitcast.99, bf16[64,64,128]{2,1,0:T(8,128)(2,1)} %get-tuple-element.25, ...), kind=kOutput, calls=%fused_computation.16 | convolution fusion | flops 1615331328 | bytes 42991624 | tf_op jit(solution)/shard_map/bij,bjc->bic/dot_general | solution.py:81
  225.0 2.1 fusion.36
  227.3 2.7 slice_negate_fusion
  230.0 4.3 pad_maximum_fusion.1
  235.0 32.0 %gather_fusion.1 = bf16[1536,64,128]{2,1,0:T(8,128)(2,1)} fusion(bf16[193,64,128]{2,1,0:T(8,128)(2,1)S(1)} %concatenate.83, s32[2048]{0:T(1024)S(1)} %pad_clamp_fusion), kind=kCustom, calls=%fused_computation.1 | custom fusion | bytes 50337792 | tf_op jit(solution)/shard_map/gather | solution.py:80
  267.1 16.4 %fusion.1 = bf16[64,64,128]{2,1,0:T(8,128)(2,1)S(1)} fusion(bf16[64,64,128]{2,1,0:T(8,128)(2,1)} %bitcast.106, f32[64,64,64]{2,1,0:T(8,128)} %slice.117, f32[64,64,64]{2,1,0:T(8,128)} %slice_negate_fusion.4, bf16[64,64,1536]{2,1,0:T(8,128)(2,1)} %param.5, bf16[64,1536,128]{2,1,0:T(8,128)(2,1)} %bitcast.98, bf16[64,64,128]{2,1,0:T(8,128)(2,1)} %get-tuple-element.29, ...), kind=kOutput, calls=%fused_computation.14 | convolution fusion | flops 1615331328 | bytes 42991624 | tf_op jit(solution)/shard_map/bij,bjc->bic/dot_general | solution.py:81
  285.1 2.1 fusion.38
  291.2 6.1 %add_convert_fusion = bf16[8,4096,128]{2,1,0:T(8,128)(2,1)} fusion(f32[4096,128]{1,0:T(8,128)S(1)} %get-tuple-element.35, f32[8]{0:T(128)S(1)} %copy-done.17, f32[4096,128]{1,0:T(8,128)S(1)} %copy-done.3, f32[8]{0:T(128)S(1)} %copy-done.18, f32[4096,128]{1,0:T(8,128)S(1)} %get-tuple-element.34, f32[8]{0:T(128)S(1)} %copy-done.19, ...), kind=kLoop, calls=%fused_computation.4 | loop fusion | flops 33554432 | bytes 16777344 | tf_op jit(solution)/shard_map/convert_element_type | solution.py:101
  297.4 185.1 %reduce-scatter.2.cloned.1.call-done = bf16[1,4096,128]{2,1,0:T(8,128)(2,1)} async-done(((bf16[8,4096,128]{2,1,0:T(8,128)(2,1)}), bf16[1,4096,128]{2,1,0:T(8,128)(2,1)}) %reduce-scatter.2.cloned.1.call-update) | async-done | bytes 1048592 | tf_op jit(solution)/shard_map/reduce_scatter | solution.py:102
  484.3 25.2 %all-gather = bf16[16,128,128]{2,1,0:T(8,128)(2,1)S(1)} all-gather(bf16[1,128,128]{2,1,0:T(8,128)(2,1)S(1)} %copy.9), channel_id=2, replica_groups=mesh['quad'=8,'row'=16] {'row'}, dimensions={0}, use_global_device_ids=true | all-gather | bytes 557056 | tf_op jit(solution)/shard_map/all_gather | solution.py:13
  (84 shorter events, 24.9 us)
Async XLA Ops:
  7.2 475.2 %reduce-scatter.2.cloned.1.call-start = ((), (), s32[]{:S(2)}) async-start(), calls=%async_computation.1 | async-start | bytes 9437184 | tf_op jit(solution)/shard_map/reduce_scatter | solution.py:102
  7.2 2.2 copy-start
  7.2 2.5 copy-start.8
  10.5 19.9 %copy-start.5 = (bf16[64,128,64]{1,2,0:T(8,128)(2,1)}, bf16[64,128,64]{1,2,0:T(8,128)(2,1)S(1)}, u32[]{:S(2)}) copy-start(bf16[64,128,64]{1,2,0:T(8,128)(2,1)S(1)} %get-tuple-element.23) | copy-start | bytes 3145732
  10.5 12.8 %copy-start.16 = (s32[64,24]{0,1:T(8,128)S(1)}, s32[64,24]{0,1:T(8,128)}, u32[]{:S(2)}) copy-start(s32[64,24]{0,1:T(8,128)} %param.6) | copy-start | bytes 18436
  10.5 12.8 %copy-start.21 = (s32[64]{0:T(128)S(1)}, s32[64]{0:T(128)}, u32[]{:S(2)}) copy-start(s32[64]{0:T(128)} %param.7) | copy-start | bytes 772
  10.5 19.8 %collective-permute-start.4 = (bf16[4096,128]{1,0:T(8,128)(2,1)S(1)}, bf16[4096,128]{1,0:T(8,128)(2,1)}, u32[]{:S(2)}, u32[]{:S(2)}) collective-permute-start(bf16[4096,128]{1,0:T(8,128)(2,1)S(1)} %bitcast.109), channel_id=1, source_target_pairs={{0,1},{1,2},{2,3},{3,4},{4,5},{5,6},{6,7},{7,8},{8,9},{9,10},{10,1... | collective-permute-start | bytes 3145736 | tf_op jit(solution)/shard_map/ppermute | solution.py:26
  13.0 17.4 %collective-permute-start.5 = (bf16[4096,128]{1,0:T(8,128)(2,1)S(1)}, bf16[4096,128]{1,0:T(8,128)(2,1)}, u32[]{:S(2)}, u32[]{:S(2)}) collective-permute-start(bf16[4096,128]{1,0:T(8,128)(2,1)S(1)} %bitcast.110), channel_id=1, source_target_pairs={{1,0},{2,1},{3,2},{4,3},{5,4},{6,5},{7,6},{8,7},{9,8},{10,9},{11,1... | collective-permute-start | bytes 3145736 | tf_op jit(solution)/shard_map/ppermute | solution.py:27
  16.8 81.4 %collective-permute-start = (bf16[4096,128]{1,0:T(8,128)(2,1)}, bf16[4096,128]{1,0:T(8,128)(2,1)}, u32[]{:S(2)}, u32[]{:S(2)}) collective-permute-start(bf16[4096,128]{1,0:T(8,128)(2,1)} %bitcast.3), channel_id=1, source_target_pairs={{0,1},{1,2},{2,3},{3,4},{4,5},{5,6},{6,7},{7,8},{8,9},{9,10},{10,1... | collective-permute-start | bytes 3145736 | tf_op jit(solution)/shard_map/ppermute | solution.py:26
  21.7 76.5 %collective-permute-start.1 = (bf16[4096,128]{1,0:T(8,128)(2,1)}, bf16[4096,128]{1,0:T(8,128)(2,1)}, u32[]{:S(2)}, u32[]{:S(2)}) collective-permute-start(bf16[4096,128]{1,0:T(8,128)(2,1)} %bitcast.3), channel_id=1, source_target_pairs={{1,0},{2,1},{3,2},{4,3},{5,4},{6,5},{7,6},{8,7},{9,8},{10,9},{11,1... | collective-permute-start | bytes 3145736 | tf_op jit(solution)/shard_map/ppermute | solution.py:27
  24.7 2.8 copy-start.4
  88.1 1.2 copy-start.6
  88.1 1.9 copy-start.9
  92.6 77.8 %collective-permute-start.6 = (bf16[4096,128]{1,0:T(8,128)(2,1)}, bf16[4096,128]{1,0:T(8,128)(2,1)}, u32[]{:S(2)}, u32[]{:S(2)}) collective-permute-start(bf16[4096,128]{1,0:T(8,128)(2,1)} %bitcast.24), channel_id=1, source_target_pairs={{0,1},{1,2},{2,3},{3,4},{4,5},{5,6},{6,7},{7,8},{8,9},{9,10},{10,1... | collective-permute-start | bytes 3145736 | tf_op jit(solution)/shard_map/ppermute | solution.py:26
  96.9 73.5 %collective-permute-start.7 = (bf16[4096,128]{1,0:T(8,128)(2,1)}, bf16[4096,128]{1,0:T(8,128)(2,1)}, u32[]{:S(2)}, u32[]{:S(2)}) collective-permute-start(bf16[4096,128]{1,0:T(8,128)(2,1)} %bitcast.24), channel_id=1, source_target_pairs={{1,0},{2,1},{3,2},{4,3},{5,4},{6,5},{7,6},{8,7},{9,8},{10,9},{11,1... | collective-permute-start | bytes 3145736 | tf_op jit(solution)/shard_map/ppermute | solution.py:27
  151.6 3.0 copy-start.10
  157.7 8.7 %copy-start.7 = (f32[64,64,128]{2,1,0:T(8,128)S(1)}, f32[64,64,128]{2,1,0:T(8,128)}, u32[]{:S(2)}) copy-start(f32[64,64,128]{2,1,0:T(8,128)} %get-tuple-element.24) | copy-start | bytes 6291460
  157.7 72.3 %collective-permute-start.2 = (bf16[4096,128]{1,0:T(8,128)(2,1)}, bf16[4096,128]{1,0:T(8,128)(2,1)}, u32[]{:S(2)}, u32[]{:S(2)}) collective-permute-start(bf16[4096,128]{1,0:T(8,128)(2,1)} %bitcast.9), channel_id=1, source_target_pairs={{0,1},{1,2},{2,3},{3,4},{4,5},{5,6},{6,7},{7,8},{8,9},{9,10},{10,1... | collective-permute-start | bytes 3145736 | tf_op jit(solution)/shard_map/ppermute | solution.py:26
  162.0 68.0 %collective-permute-start.3 = (bf16[4096,128]{1,0:T(8,128)(2,1)}, bf16[4096,128]{1,0:T(8,128)(2,1)}, u32[]{:S(2)}, u32[]{:S(2)}) collective-permute-start(bf16[4096,128]{1,0:T(8,128)(2,1)} %bitcast.9), channel_id=1, source_target_pairs={{1,0},{2,1},{3,2},{4,3},{5,4},{6,5},{7,6},{8,7},{9,8},{10,9},{11,1... | collective-permute-start | bytes 3145736 | tf_op jit(solution)/shard_map/ppermute | solution.py:27
  223.4 1.6 copy-start.11
  227.3 2.7 copy-start.2
  283.5 1.6 copy-start.12
  287.4 1.6 copy-start.13
  287.4 2.2 copy-start.14
  289.6 1.6 copy-start.3
  289.6 1.6 copy-start.17
  289.6 1.6 copy-start.18
  289.6 1.6 copy-start.19
  289.6 1.6 copy-start.20
  297.3 185.1 %copy-start.1 = (bf16[4096,128]{1,0:T(8,128)(2,1)S(1)}, bf16[4096,128]{1,0:T(8,128)(2,1)}, u32[]{:S(2)}) copy-start(bf16[4096,128]{1,0:T(8,128)(2,1)} %param.9) | copy-start | bytes 3145732
  482.4 28.1 %copy-start.15 = (bf16[1,4096,128]{2,1,0:T(8,128)(2,1)S(1)}, bf16[1,4096,128]{2,1,0:T(8,128)(2,1)}, u32[]{:S(2)}) copy-start(bf16[1,4096,128]{2,1,0:T(8,128)(2,1)} %reduce-scatter.2.cloned.1.call-done) | copy-start | bytes 3145732
Sparse Core Ops, SparseCore 0:
  297.5 184.8 reduce-scatter.1
